TPU v7x, 128 devices: a whole 4x4x4 slice. The times are simulated.
128 devices in a mesh: front: 4 (over y), rows: 32 (over z, x, core).
Axes of the slice: x: 4, y: 4, z: 4, core: 2. Of those that a mesh axis runs over, the one named last changes fastest.
Arguments:
- panel_g: bfloat16 [4, 32, 2048, 256], P('front', 'rows'), may hold values from -6 to 6
- refl_root: bfloat16 [4, 32, 2048, 512], P('front', 'rows'), may hold values from -6 to 6
- refl_mid: bfloat16 [4, 32, 4096, 512], P('front', 'rows'), may hold values from -6 to 6
- refl_leaf: bfloat16 [4, 32, 4096, 512], P('front', 'rows'), may hold values from -6 to 6
- tri_root: float32 [512, 512], replicated, as said below
- tri_mid: float32 [4, 512, 512], P('front'), as said below
- tri_leaf: float32 [4, 512, 512], P('front'), as said below
- route_root: int32 [4, 32, 16], P('front', 'rows'), may hold values from 0 to 3, as said below
- route_mid: int32 [4, 32, 32], P('front', 'rows'), may hold values from 0 to 3, as said below
Outputs:
- leaf_g: bfloat16 [4, 32, 4096, 256], P('front', 'rows')
Inputs may be any that keep to these rules, and one draw needn't show every extreme that they name: `route_root`: on every device at most 8 blocks name the same front, and some front is named by exactly 8 of them. `route_mid`: on every device each front is named by exactly 8 slots. `tri_root`: upper triangular. `tri_mid`: upper triangular. `tri_leaf`: upper triangular.
All inputs are finite; a program needn't handle non-finite values.
Results may differ from a plain program's by a relative error of at most 0.01.
Values may be sent and summed in bfloat16 or wider, within the bound.
No kernel may reach another device: no remote copies, remote signals or barrier semaphores. Data moves between devices by JAX's collectives and lax.ppermute only.
A program may use at most 64 MiB of HBM per device.

v0:
```python
import jax
import jax.numpy as jnp
from jax import lax
from jax.experimental import pallas as pl
from jax.experimental.pallas import tpu as pltpu
from jax.sharding import Mesh
from jax.sharding import PartitionSpec as P

BLOCK = 128
FRONTS = 4
CAP = 8
COLS = 256
REFL = 512
CHUNK = CAP * BLOCK
FLAGS = 16
TILE = 512
ROWS = ("rows_0", "rows_1", "rows_2")
ALL = ("front",) + ROWS
F32 = jnp.float32
BF16 = jnp.bfloat16


def row_sums(panel, refl):
    return lax.dot_general(panel, refl, (((0,), (0,)), ((), ())), preferred_element_type=F32)


def times_coeffs(refl, coeffs_t):
    return lax.dot_general(refl, coeffs_t, (((1,), (1,)), ((), ())), preferred_element_type=F32)


VMEM = pl.BlockSpec(memory_space=pltpu.VMEM)
SMEM = pl.BlockSpec(memory_space=pltpu.SMEM)
HBM = pl.BlockSpec(memory_space=pltpu.MemorySpace.HBM)
DMA = pltpu.SemaphoreType.DMA


def local_call(kernel, name, outs, held=(), numbers=(), far=(), scratch=()):
    held = [pltpu.with_memory_space_constraint(a, pltpu.VMEM) for a in held]
    far = [pltpu.with_memory_space_constraint(a, pltpu.MemorySpace.HBM) for a in far]
    with jax.named_scope(name):
        return pl.pallas_call(
            kernel,
            in_specs=[SMEM] * len(numbers) + [VMEM] * len(held) + [HBM] * len(far),
            out_specs=[spec for spec, _ in outs],
            out_shape=[shape for _, shape in outs],
            scratch_shapes=list(scratch),
            compiler_params=pltpu.CompilerParams(vmem_limit_bytes=12 << 20),
            name=name,
        )(*numbers, *held, *far)


def in_vmem(shape, dtype=BF16):
    return VMEM, pltpu.VMEM(shape, dtype)


def in_smem(count):
    return SMEM, jax.ShapeDtypeStruct((count,), jnp.int32)


def rows_at(block, count=1):
    return pl.ds(pl.multiple_of(block * BLOCK, BLOCK), count * BLOCK)


def root_partial(panel, refl, route_root, route_mid):
    rows = panel.shape[0]
    steps = rows // TILE
    slots = FRONTS * CAP

    def place_blocks(route_ref, table_ref, seen_ref):
        for goal in range(FRONTS):
            seen_ref[goal] = 0

        def body(i, _):
            goal = route_ref[i]
            table_ref[goal * CAP + seen_ref[goal]] = i
            seen_ref[goal] = seen_ref[goal] + 1
            return 0

        lax.fori_loop(0, route_ref.shape[0], body, 0)

    def kernel(
        g_far, y_far, r0_far, r1_far, out_ref, g_ref, y_ref, t0_ref, t1_ref, tall_ref, acc_ref, seen_ref, r0_ref, r1_ref, sems, route_sems
    ):
        routes = [
            pltpu.make_async_copy(r0_far, r0_ref, route_sems.at[0]),
            pltpu.make_async_copy(r1_far, r1_ref, route_sems.at[1]),
        ]
        for copy in routes:
            copy.start()

        def copies(i):
            at = pl.ds(i * TILE, TILE)
            return [
                pltpu.make_async_copy(far.at[at], near.at[at], sems.at[k, i])
                for k, (far, near) in enumerate(((y_far, y_ref), (g_far, g_ref)))
            ]

        for i in range(steps):
            for copy in copies(i):
                copy.start()
        for i in range(slots):
            t0_ref[i] = -1
        for copy in routes:
            copy.wait()
        place_blocks(r0_ref, t0_ref, seen_ref)
        place_blocks(r1_ref, t1_ref, seen_ref)
        for i in range(steps):
            for copy in copies(i):
                copy.wait()
            at = slice(i * TILE, (i + 1) * TILE)
            part = row_sums(g_ref[at, :], y_ref[at, :])
            acc_ref[...] = part if i == 0 else acc_ref[...] + part
        for j in range(4):
            tall_ref[pl.ds(j, COLS, stride=4), :] = acc_ref[:, 128 * j : 128 * (j + 1)]
        out_ref[...] = tall_ref[...].astype(BF16)

    return local_call(
        kernel,
        "root_partial",
        [in_vmem((COLS * 4, 128)), in_vmem((rows, COLS)), in_vmem((rows, REFL))]
        + [in_smem(slots), in_smem(slots)],
        far=[panel, refl, route_root, route_mid],
        scratch=[
            pltpu.VMEM((COLS * 4, 128), F32),
            pltpu.VMEM((COLS, REFL), F32),
            pltpu.SMEM((FRONTS,), jnp.int32),
            pltpu.SMEM(route_root.shape, jnp.int32),
            pltpu.SMEM(route_mid.shape, jnp.int32),
            DMA((2, steps)),
            DMA((2,)),
        ],
    )


def front_partial(chunks, refl):
    def kernel(g_ref, y_ref, out_ref, acc_ref):
        for f in range(FRONTS):
            part = row_sums(g_ref[f, :CHUNK, :], y_ref[f * CHUNK : (f + 1) * CHUNK, :])
            acc_ref[...] = part if f == 0 else acc_ref[...] + part
        out_ref[...] = acc_ref[...].astype(BF16)

    return local_call(
        kernel,
        "front_partial",
        [in_vmem((COLS, REFL))],
        [chunks, refl],
        scratch=[pltpu.VMEM((COLS, REFL), F32)],
    )[0]


def split_bf16(x):
    high = x.astype(BF16)
    return high, (x - high.astype(F32)).astype(BF16)


def fine_dot(a, b):
    a_high, a_low = split_bf16(a)
    b_high, b_low = split_bf16(b)
    dot = lambda u, v: jnp.dot(u, v, preferred_element_type=F32)
    return dot(a_high, b_high) + (dot(a_low, b_high) + dot(a_high, b_low))


def root_share(arrived, triangle):
    def kernel(x_ref, t_ref, out_ref):
        total = jnp.sum(x_ref[...].astype(F32), axis=0)
        rows = [jnp.concatenate([total[4 * c + j : 4 * c + j + 1] for j in range(4)], 1) for c in range(2)]
        both = jnp.concatenate(rows + [jnp.zeros((6, REFL), F32)], axis=0)
        coeffs = fine_dot(both, t_ref[...])
        chunk = jnp.concatenate(
            [coeffs[c : c + 1, 128 * j : 128 * (j + 1)] for c in range(2) for j in range(4)], 0
        )
        out_ref[...] = jnp.broadcast_to(chunk.astype(BF16)[None], out_ref.shape)

    return local_call(kernel, "root_share", [in_vmem(arrived.shape)], [arrived, triangle])[0]


def front_share(arrived, triangle):
    def kernel(x_ref, t_ref, out_ref):
        total = jnp.sum(x_ref[...].astype(F32), axis=0)
        coeffs = fine_dot(total, t_ref[...]).astype(BF16)
        out_ref[...] = jnp.broadcast_to(coeffs[None], out_ref.shape)

    return local_call(kernel, "front_share", [in_vmem(arrived.shape)], [arrived, triangle])[0]


LEAVING = in_vmem((FRONTS, CHUNK + FLAGS, COLS))


def root_apply(coeffs, panel, refl, table):
    blocks = panel.shape[0] // BLOCK

    def kernel(t_ref, c_ref, g_ref, y_ref, out_ref, tall_ref, ct_ref, new_ref):
        tall_ref[...] = c_ref[...].astype(F32)
        for j in range(4):
            ct_ref[:, 128 * j : 128 * (j + 1)] = tall_ref[pl.ds(j, COLS, stride=4), :].astype(BF16)
        for i in range(blocks * BLOCK // TILE):
            at = slice(i * TILE, (i + 1) * TILE)
            new = g_ref[at, :].astype(F32) - times_coeffs(y_ref[at, :], ct_ref[...])
            new_ref[at, :] = new.astype(BF16)
        row = lax.broadcasted_iota(jnp.int32, (FLAGS, COLS), 0)
        for f in range(FRONTS):
            flags = jnp.zeros((FLAGS, COLS), F32)
            for p in range(CAP):
                at = t_ref[f * CAP + p]
                block = new_ref[rows_at(jnp.maximum(at, 0)), :]
                out_ref[f, p * BLOCK : (p + 1) * BLOCK, :] = jnp.where(at >= 0, block, jnp.zeros_like(block))
                flags = jnp.where((row == p) & (at >= 0), 1.0, flags)
            out_ref[f, CHUNK:, :] = flags.astype(BF16)

    return local_call(
        kernel,
        "root_apply",
        [LEAVING],
        [coeffs, panel, refl],
        [table],
        scratch=[
            pltpu.VMEM((COLS * 4, 128), F32),
            pltpu.VMEM((COLS, REFL), BF16),
            pltpu.VMEM(panel.shape, BF16),
        ],
    )[0]


def updated(c_ref, g_ref, y_ref, write, after=lambda f, i: None):
    per = TILE // BLOCK
    for f in range(FRONTS):
        flags = g_ref[f, CHUNK:, :].astype(F32)
        for i in range(CAP // per):
            at = f * CHUNK + i * TILE
            update = times_coeffs(y_ref[at : at + TILE, :], c_ref[...])
            for b in range(per):
                p = i * per + b
                old = g_ref[f, p * BLOCK : (p + 1) * BLOCK, :].astype(F32)
                new = (old - update[b * BLOCK : (b + 1) * BLOCK, :]) * flags[p : p + 1, :]
                write(f * CAP + p, new.astype(BF16))
            after(f, i)


def front_apply(coeffs, chunks, refl, table):
    def kernel(t_ref, c_ref, g_ref, y_ref, out_ref, new_ref, flag_ref):
        def write(slot, value):
            new_ref[slot * BLOCK : (slot + 1) * BLOCK, :] = value

        updated(c_ref, g_ref, y_ref, write)
        for f in range(FRONTS):
            flag_ref[f * CAP : (f + 1) * CAP, :] = g_ref[f, CHUNK:, :].astype(F32)[:CAP]
        for f in range(FRONTS):
            rows = []
            for p in range(CAP):
                at = t_ref[f * CAP + p]
                out_ref[f, p * BLOCK : (p + 1) * BLOCK, :] = new_ref[rows_at(at), :]
                rows.append(flag_ref[pl.ds(at, 1), :])
            rows.append(jnp.zeros((FLAGS - CAP, COLS), F32))
            out_ref[f, CHUNK:, :] = jnp.concatenate(rows, axis=0).astype(BF16)

    return local_call(
        kernel,
        "front_apply",
        [LEAVING],
        [coeffs, chunks, refl],
        [table],
        scratch=[pltpu.VMEM((FRONTS * CHUNK, COLS), BF16), pltpu.VMEM((FRONTS * CAP, COLS), F32)],
    )[0]


def leaf_apply(coeffs, chunks, refl):
    per = CHUNK // TILE

    def kernel(c_ref, g_ref, y_ref, out_far, new_ref, sems):
        def write(slot, value):
            new_ref[slot * BLOCK : (slot + 1) * BLOCK, :] = value

        def leave(f, i):
            at = pl.ds((f * per + i) * TILE, TILE)
            return pltpu.make_async_copy(new_ref.at[at], out_far.at[at], sems.at[f * per + i])

        updated(c_ref, g_ref, y_ref, write, lambda f, i: leave(f, i).start())
        for f in range(FRONTS):
            for i in range(per):
                leave(f, i).wait()

    return local_call(
        kernel,
        "leaf_apply",
        [(HBM, jax.ShapeDtypeStruct((FRONTS * CHUNK, COLS), BF16))],
        [coeffs, chunks, refl],
        scratch=[pltpu.VMEM((FRONTS * CHUNK, COLS), BF16), DMA((FRONTS * per,))],
    )[0]


def all_to_all(x, axes):
    return lax.all_to_all(x, axes, 0, 0, tiled=True)


def front_level(chunks, refl, triangle):
    partial = front_partial(chunks, refl)
    arrived = all_to_all(partial.reshape(32, COLS // 32, REFL), ROWS)
    return all_to_all(front_share(arrived, triangle), ROWS).reshape(COLS, REFL)


def per_device(
    panel_g, refl_root, refl_mid, refl_leaf, tri_root, tri_mid, tri_leaf, route_root, route_mid
):
    panel = panel_g.reshape(-1, COLS)
    y_root, y_mid, y_leaf = (y.reshape(-1, REFL) for y in (refl_root, refl_mid, refl_leaf))

    partial, panel, y_root, root_table, mid_table = root_partial(
        panel, y_root, route_root.reshape(-1), route_mid.reshape(-1)
    )
    arrived = all_to_all(partial.reshape(128, 8, 128), ALL)
    coeffs = all_to_all(root_share(arrived, tri_root), ALL).reshape(COLS * 4, 128)
    chunks = all_to_all(root_apply(coeffs, panel, y_root, root_table), "front")

    coeffs = front_level(chunks, y_mid, tri_mid[0])
    chunks = all_to_all(front_apply(coeffs, chunks, y_mid, mid_table), "front")

    coeffs = front_level(chunks, y_leaf, tri_leaf[0])
    out = leaf_apply(coeffs, chunks, y_leaf)
    return out.reshape(refl_leaf.shape[:3] + (COLS,))


def solution(mesh):
    finer = Mesh(
        mesh.devices.reshape(mesh.shape["front"], 4, 4, 2), ("front", "rows_0", "rows_1", "rows_2")
    )
    rows = P("front", ROWS, None, None)
    placed = (
        rows,
        rows,
        rows,
        rows,
        P(),
        P("front", None, None),
        P("front", None, None),
        P("front", ROWS, None),
        P("front", ROWS, None),
    )
    return jax.shard_map(
        per_device,
        mesh=finer,
        in_specs=placed,
        out_specs=rows,
        check_vma=False,
    )
```

profile of v0, /device:TPU:1, one launch (start us, length us, event | category | flops | bytes accessed | tf_op | source)
XLA Modules:
  0.0 160.2 jit_solution(4430512394015174194)
XLA Ops:
  0.0 0.0 copy-start.2
  0.0 2.8 %root_partial.1 = (bf16[1024,128]{1,0:T(8,128)(2,1)S(1)}, bf16[2048,256]{1,0:T(8,128)(2,1)S(1)}, bf16[2048,512]{1,0:T(8,128)(2,1)S(1)}, s32[32]{0:T(128)S(1)}, s32[32]{0:T(128)S(1)}) custom-call(bf16[2048,256]{1,0:T(8,128)(2,1)} %bitcast.28, bf16[2048,512]{1,0:T(8,128)(2,1)} %bitcast.27, s32[16]{0:T(128)} %bitcast.29, s32[32]{0:T(128)} %bitcast.30), custom_call_target="tpu_custom_call" | custom-call | tf_op jit(solution)/shard_map/root_partial/root_partial/pallas_call | solution.py:41
  2.8 22.2 %all_to_all.40.x_ref = bf16[128,8,128]{2,1,0:T(8,128)(2,1)S(1)} all-to-all(bf16[128,8,128]{2,1,0:T(8,128)(2,1)S(1)} %bitcast.26), channel_id=1, replica_groups=mesh['front'=4,'rows_0'=4,'rows_1'=4,'rows_2'=2] {'front','rows_0','rows..., dimensions={0} | all-to-all | bytes 524288 | tf_op jit(solution)/shard_map/all_to_all | solution.py:292
  24.9 0.0 copy-done.2
  24.9 0.5 root_share.1
  25.4 15.3 %all_to_all.41 = bf16[128,8,128]{2,1,0:T(8,128)(2,1)S(1)} all-to-all(bf16[128,8,128]{2,1,0:T(8,128)(2,1)S(1)} %root_share.1), channel_id=1, replica_groups=mesh['front'=4,'rows_0'=4,'rows_1'=4,'rows_2'=2] {'front','rows_0','rows..., dimensions={0} | all-to-all | bytes 524288 | tf_op jit(solution)/shard_map/all_to_all | solution.py:292
  40.7 1.6 %root_apply.1 = bf16[4,1040,256]{2,1,0:T(8,128)(2,1)S(1)} custom-call(s32[32]{0:T(128)S(1)} %get-tuple-element.11.t_ref, bf16[1024,128]{1,0:T(8,128)(2,1)S(1)} %bitcast.19, bf16[2048,256]{1,0:T(8,128)(2,1)S(1)} %get-tuple-element.13.g_ref, bf16[2048,512]{1,0:T(8,128)(2,1)S(1)} %get-tuple-element.14.y_ref), custom_call_target="tpu_custom_call" | custom-call | tf_op jit(solution)/shard_map/root_apply/root_apply/pallas_call | solution.py:41
  42.4 0.0 copy-start
  42.4 28.3 %all_to_all.42.g_ref = bf16[4,1040,256]{2,1,0:T(8,128)(2,1)S(1)} all-to-all(bf16[4,1040,256]{2,1,0:T(8,128)(2,1)S(1)} %root_apply.1), channel_id=1, replica_groups=mesh['front'=4,'rows_0'=4,'rows_1'=4,'rows_2'=2] {'front'}, dimensions={0} | all-to-all | bytes 4259840 | tf_op jit(solution)/shard_map/all_to_all | solution.py:292
  70.7 0.0 copy-done
  70.7 0.0 copy-start.3
  70.7 1.3 front_partial.2
  72.0 14.5 %all_to_all.43.x_ref = bf16[32,8,512]{2,1,0:T(8,128)(2,1)S(1)} all-to-all(bf16[32,8,512]{2,1,0:T(8,128)(2,1)S(1)} %bitcast.22), channel_id=1, replica_groups=mesh['front'=4,'rows_0'=4,'rows_1'=4,'rows_2'=2] {'rows_0','rows_1','row..., dimensions={0} | all-to-all | bytes 524288 | tf_op jit(solution)/shard_map/all_to_all | solution.py:292
  86.5 0.0 copy-done.3
  86.5 0.4 front_share.2
  86.9 12.4 %all_to_all.44 = bf16[32,8,512]{2,1,0:T(8,128)(2,1)S(1)} all-to-all(bf16[32,8,512]{2,1,0:T(8,128)(2,1)S(1)} %front_share.2), channel_id=1, replica_groups=mesh['front'=4,'rows_0'=4,'rows_1'=4,'rows_2'=2] {'rows_0','rows_1','row..., dimensions={0} | all-to-all | bytes 524288 | tf_op jit(solution)/shard_map/all_to_all | solution.py:292
  99.4 2.0 %front_apply.1 = bf16[4,1040,256]{2,1,0:T(8,128)(2,1)S(1)} custom-call(s32[32]{0:T(128)S(1)} %get-tuple-element.10.t_ref, bf16[256,512]{1,0:T(8,128)(2,1)S(1)} %bitcast.20, bf16[4,1040,256]{2,1,0:T(8,128)(2,1)S(1)} %all_to_all.42.g_ref, bf16[4096,512]{1,0:T(8,128)(2,1)S(1)} %bitcast.16), custom_call_target="tpu_custom_call" | custom-call | tf_op jit(solution)/shard_map/front_apply/front_apply/pallas_call | solution.py:41
  101.3 0.0 copy-start.1
  101.4 29.0 %all_to_all.45.g_ref = bf16[4,1040,256]{2,1,0:T(8,128)(2,1)S(1)} all-to-all(bf16[4,1040,256]{2,1,0:T(8,128)(2,1)S(1)} %front_apply.1), channel_id=1, replica_groups=mesh['front'=4,'rows_0'=4,'rows_1'=4,'rows_2'=2] {'front'}, dimensions={0} | all-to-all | bytes 4259840 | tf_op jit(solution)/shard_map/all_to_all | solution.py:292
  130.4 0.0 copy-done.1
  130.4 0.0 copy-start.4
  130.4 1.3 front_partial.3
  131.7 13.4 %all_to_all.46.x_ref = bf16[32,8,512]{2,1,0:T(8,128)(2,1)S(1)} all-to-all(bf16[32,8,512]{2,1,0:T(8,128)(2,1)S(1)} %bitcast.23), channel_id=1, replica_groups=mesh['front'=4,'rows_0'=4,'rows_1'=4,'rows_2'=2] {'rows_0','rows_1','row..., dimensions={0} | all-to-all | bytes 524288 | tf_op jit(solution)/shard_map/all_to_all | solution.py:292
  145.1 0.0 copy-done.4
  145.1 0.4 front_share.3
  145.5 12.4 %all_to_all.47 = bf16[32,8,512]{2,1,0:T(8,128)(2,1)S(1)} all-to-all(bf16[32,8,512]{2,1,0:T(8,128)(2,1)S(1)} %front_share.3), channel_id=1, replica_groups=mesh['front'=4,'rows_0'=4,'rows_1'=4,'rows_2'=2] {'rows_0','rows_1','row..., dimensions={0} | all-to-all | bytes 524288 | tf_op jit(solution)/shard_map/all_to_all | solution.py:292
  158.0 2.2 %leaf_apply.1 = bf16[4096,256]{1,0:T(8,128)(2,1)} custom-call(bf16[256,512]{1,0:T(8,128)(2,1)S(1)} %bitcast.21, bf16[4,1040,256]{2,1,0:T(8,128)(2,1)S(1)} %all_to_all.45.g_ref, bf16[4096,512]{1,0:T(8,128)(2,1)S(1)} %bitcast.18), custom_call_target="tpu_custom_call" | custom-call | tf_op jit(solution)/shard_map/leaf_apply/leaf_apply/pallas_call | solution.py:41
Async XLA Ops:
  0.0 24.9 %copy-start.2 = (f32[512,512]{1,0:T(8,128)S(1)}, f32[512,512]{1,0:T(8,128)}, u32[]{:S(2)}) copy-start(f32[512,512]{1,0:T(8,128)} %t_ref.1) | copy-start | bytes 3145732
  42.4 28.3 %copy-start = (bf16[1,1,4096,512]{3,2,1,0:T(8,128)(2,1)S(1)}, bf16[1,1,4096,512]{3,2,1,0:T(8,128)(2,1)}, u32[]{:S(2)}) copy-start(bf16[1,1,4096,512]{3,2,1,0:T(8,128)(2,1)} %param.11) | copy-start | bytes 12582916
  70.7 15.8 %copy-start.3 = (f32[1,512,512]{2,1,0:T(8,128)S(1)}, f32[1,512,512]{2,1,0:T(8,128)}, u32[]{:S(2)}) copy-start(f32[1,512,512]{2,1,0:T(8,128)} %param.14) | copy-start | bytes 3145732
  101.3 29.1 %copy-start.1 = (bf16[1,1,4096,512]{3,2,1,0:T(8,128)(2,1)S(1)}, bf16[1,1,4096,512]{3,2,1,0:T(8,128)(2,1)}, u32[]{:S(2)}) copy-start(bf16[1,1,4096,512]{3,2,1,0:T(8,128)(2,1)} %param.12) | copy-start | bytes 12582916
  130.4 14.7 %copy-start.4 = (f32[1,512,512]{2,1,0:T(8,128)S(1)}, f32[1,512,512]{2,1,0:T(8,128)}, u32[]{:S(2)}) copy-start(f32[1,512,512]{2,1,0:T(8,128)} %param.15) | copy-start | bytes 3145732
where the time goes:
time: 161 us; the launch traced here: 160 us
  blocking collectives  148 us (92%)
  Pallas kernels  12.4 us (8%)
    all_to_all x8, blocking collectives, all_to_all(): return lax.all_to_all(x, axes, 0, 0, tiled=True)  148 us
    pallas_call x9, Pallas kernels, local_call(): pl.pallas_call(kernel, in_specs=[SMEM] * len(numbers) + [VMEM] * len(held...  12.4 us

commit v1 on v0

v1 whole, which is shorter than its diff:
```python
import jax
import jax.numpy as jnp
from jax import lax
from jax.experimental import pallas as pl
from jax.experimental.pallas import tpu as pltpu
from jax.sharding import Mesh
from jax.sharding import PartitionSpec as P


BLOCK = 128
FRONTS = 4
CAP = 8
COLS = 256
REFL = 512
CHUNK = CAP * BLOCK
FLAGS = 16
TILE = 512
ROWS = ("rows_0", "rows_1", "rows_2")
ALL = ("front",) + ROWS
F32 = jnp.float32
BF16 = jnp.bfloat16


def row_sums(panel, refl):
    return lax.dot_general(panel, refl, (((0,), (0,)), ((), ())), preferred_element_type=F32)


def times_coeffs(refl, coeffs_t):
    return lax.dot_general(refl, coeffs_t, (((1,), (1,)), ((), ())), preferred_element_type=F32)


VMEM = pl.BlockSpec(memory_space=pltpu.VMEM)
SMEM = pl.BlockSpec(memory_space=pltpu.SMEM)
HBM = pl.BlockSpec(memory_space=pltpu.MemorySpace.HBM)
DMA = pltpu.SemaphoreType.DMA


def local_call(kernel, outs, held=(), numbers=(), far=(), scratch=()):
    held = [pltpu.with_memory_space_constraint(a, pltpu.VMEM) for a in held]
    far = [pltpu.with_memory_space_constraint(a, pltpu.MemorySpace.HBM) for a in far]
    return pl.pallas_call(
        kernel,
        in_specs=[SMEM] * len(numbers) + [VMEM] * len(held) + [HBM] * len(far),
        out_specs=[spec for spec, _ in outs],
        out_shape=[shape for _, shape in outs],
        scratch_shapes=list(scratch),
        compiler_params=pltpu.CompilerParams(vmem_limit_bytes=12 << 20),
    )(*numbers, *held, *far)


def in_vmem(shape, dtype=BF16):
    return VMEM, pltpu.VMEM(shape, dtype)


def in_smem(count):
    return SMEM, jax.ShapeDtypeStruct((count,), jnp.int32)


def rows_at(block, count=1):
    return pl.ds(pl.multiple_of(block * BLOCK, BLOCK), count * BLOCK)


def root_partial(panel, refl, route_root, route_mid):
    rows = panel.shape[0]
    steps = rows // TILE
    slots = FRONTS * CAP

    def place_blocks(route_ref, table_ref, seen_ref):
        for goal in range(FRONTS):
            seen_ref[goal] = 0

        def body(i, _):
            goal = route_ref[i]
            table_ref[goal * CAP + seen_ref[goal]] = i
            seen_ref[goal] = seen_ref[goal] + 1
            return 0

        lax.fori_loop(0, route_ref.shape[0], body, 0)

    def kernel(
        g_far, y_far, r0_far, r1_far, out_ref, g_ref, y_ref, t0_ref, t1_ref, tall_ref, acc_ref, seen_ref, r0_ref, r1_ref, sems, route_sems
    ):
        routes = [
            pltpu.make_async_copy(r0_far, r0_ref, route_sems.at[0]),
            pltpu.make_async_copy(r1_far, r1_ref, route_sems.at[1]),
        ]
        for copy in routes:
            copy.start()

        def copies(i):
            at = pl.ds(i * TILE, TILE)
            return [
                pltpu.make_async_copy(far.at[at], near.at[at], sems.at[k, i])
                for k, (far, near) in enumerate(((y_far, y_ref), (g_far, g_ref)))
            ]

        for i in range(steps):
            for copy in copies(i):
                copy.start()
        for i in range(slots):
            t0_ref[i] = -1
        for copy in routes:
            copy.wait()
        place_blocks(r0_ref, t0_ref, seen_ref)
        place_blocks(r1_ref, t1_ref, seen_ref)
        for i in range(steps):
            for copy in copies(i):
                copy.wait()
            at = slice(i * TILE, (i + 1) * TILE)
            part = row_sums(g_ref[at, :], y_ref[at, :])
            acc_ref[...] = part if i == 0 else acc_ref[...] + part
        for j in range(4):
            tall_ref[pl.ds(j, COLS, stride=4), :] = acc_ref[:, 128 * j : 128 * (j + 1)]
        out_ref[...] = tall_ref[...].astype(BF16)

    return local_call(
        kernel,
        [in_vmem((COLS * 4, 128)), in_vmem((rows, COLS)), in_vmem((rows, REFL))]
        + [in_smem(slots), in_smem(slots)],
        far=[panel, refl, route_root, route_mid],
        scratch=[
            pltpu.VMEM((COLS * 4, 128), F32),
            pltpu.VMEM((COLS, REFL), F32),
            pltpu.SMEM((FRONTS,), jnp.int32),
            pltpu.SMEM(route_root.shape, jnp.int32),
            pltpu.SMEM(route_mid.shape, jnp.int32),
            DMA((2, steps)),
            DMA((2,)),
        ],
    )


def ring_index(shift):
    return jnp.bitwise_and(lax.axis_index("front") + shift, FRONTS - 1)


def staged(refl, after):
    def kernel(after_ref, y_far, y_ref, sem):
        copy = pltpu.make_async_copy(y_far, y_ref, sem.at[0])
        copy.start()
        copy.wait()

    return local_call(
        kernel, [in_vmem(refl.shape)], numbers=[after], far=[refl], scratch=[DMA((1,))]
    )[0]


def front_partial(chunks, refl, before, last):
    shifts = list(chunks)
    ahead = [] if before is None else [before]

    def kernel(*refs):
        y_ref, out_ref, acc_ref = refs[-3], refs[-2], refs[-1]
        total = acc_ref if last else out_ref
        for k, d in enumerate(shifts):
            rows = y_ref[rows_at(ring_index(-d) * CAP, CAP), :]
            part = row_sums(refs[k][:CHUNK, :], rows)
            if k == 0 and before is not None:
                part = part + refs[len(shifts)][...]
            total[...] = part if k == 0 else total[...] + part
        if last:
            out_ref[...] = acc_ref[...].astype(BF16)

    return local_call(
        kernel,
        [in_vmem((COLS, REFL), BF16 if last else F32)],
        [*chunks.values(), *ahead, refl],
        scratch=[pltpu.VMEM((COLS, REFL), F32)],
    )[0]


def split_bf16(x):
    high = x.astype(BF16)
    return high, (x - high.astype(F32)).astype(BF16)


def fine_dot(a, b):
    a_high, a_low = split_bf16(a)
    b_high, b_low = split_bf16(b)
    dot = lambda u, v: jnp.dot(u, v, preferred_element_type=F32)
    return dot(a_high, b_high) + (dot(a_low, b_high) + dot(a_high, b_low))


def root_share(arrived, triangle):
    def kernel(x_ref, t_ref, out_ref):
        total = jnp.sum(x_ref[...].astype(F32), axis=0)
        rows = [jnp.concatenate([total[4 * c + j : 4 * c + j + 1] for j in range(4)], 1) for c in range(2)]
        both = jnp.concatenate(rows + [jnp.zeros((6, REFL), F32)], axis=0)
        coeffs = fine_dot(both, t_ref[...])
        chunk = jnp.concatenate(
            [coeffs[c : c + 1, 128 * j : 128 * (j + 1)] for c in range(2) for j in range(4)], 0
        )
        out_ref[...] = jnp.broadcast_to(chunk.astype(BF16)[None], out_ref.shape)

    return local_call(kernel, [in_vmem(arrived.shape)], [arrived, triangle])[0]


def front_share(arrived, triangle):
    def kernel(x_ref, t_ref, out_ref):
        total = jnp.sum(x_ref[...].astype(F32), axis=0)
        coeffs = fine_dot(total, t_ref[...]).astype(BF16)
        out_ref[...] = jnp.broadcast_to(coeffs[None], out_ref.shape)

    return local_call(kernel, [in_vmem(arrived.shape)], [arrived, triangle])[0]


LEAVING = in_vmem((CHUNK + FLAGS, COLS))
GATHERED = [pltpu.VMEM((CHUNK, REFL), BF16), pltpu.VMEM((CHUNK, COLS), F32)]


def leave(shift, table_ref, pick_panel, pick_flag, y_ref, ct_ref, out_ref, ys_ref, gs_ref):
    goal = ring_index(shift) * CAP
    flags = []
    for p in range(CAP):
        at = table_ref[goal + p]
        block = jnp.maximum(at, 0)
        here = slice(p * BLOCK, (p + 1) * BLOCK)
        ys_ref[here, :] = y_ref[rows_at(block), :]
        pick_panel(block, gs_ref, here)
        flags.append(pick_flag(at))
    for i in range(CHUNK // TILE):
        at = slice(i * TILE, (i + 1) * TILE)
        update = times_coeffs(ys_ref[at, :], ct_ref[...])
        for b in range(TILE // BLOCK):
            p = i * (TILE // BLOCK) + b
            here = slice(p * BLOCK, (p + 1) * BLOCK)
            new = (gs_ref[here, :] - update[b * BLOCK : (b + 1) * BLOCK, :]) * flags[p]
            out_ref[here, :] = new.astype(BF16)
    rows = flags + [jnp.zeros((FLAGS - CAP, COLS), F32)]
    out_ref[CHUNK:, :] = jnp.concatenate(rows, axis=0).astype(BF16)


def root_leave(shift, coeffs, panel, refl, table, first):
    def kernel(t_ref, c_ref, g_ref, y_ref, out_ref, *rest):
        if first:
            ct_ref, token_ref, tall_ref, ys_ref, gs_ref = rest
            token_ref[0] = 0
            tall_ref[...] = c_ref[...].astype(F32)
            for j in range(4):
                ct_ref[:, 128 * j : 128 * (j + 1)] = tall_ref[pl.ds(j, COLS, stride=4), :].astype(BF16)
        else:
            ct_ref, (ys_ref, gs_ref) = c_ref, rest

        def pick_panel(block, to_ref, here):
            to_ref[here, :] = g_ref[rows_at(block), :].astype(F32)

        def pick_flag(at):
            return jnp.broadcast_to(jnp.where(at >= 0, 1.0, 0.0).astype(F32), (1, COLS))

        leave(shift, t_ref, pick_panel, pick_flag, y_ref, ct_ref, out_ref, ys_ref, gs_ref)

    return local_call(
        kernel,
        [LEAVING] + ([in_vmem((COLS, REFL)), in_smem(1)] if first else []),
        [coeffs, panel, refl],
        [table],
        scratch=([pltpu.VMEM((COLS * 4, 128), F32)] if first else []) + GATHERED,
    )


def front_leave(shift, coeffs, chunks, refl, table, first):
    def kernel(t_ref, c_ref, g0, g1, g2, g3, y_ref, out_ref, *rest):
        *token, ys_ref, gs_ref, flag_ref = rest
        for token_ref in token:
            token_ref[0] = 0
        for d, g_ref in enumerate((g0, g1, g2, g3)):
            flag_ref[d * FLAGS : (d + 1) * FLAGS, :] = g_ref[CHUNK:, :].astype(F32)

        def chunk_of(block):
            return ring_index(-(block // CAP)), block % CAP

        def pick_panel(block, to_ref, here):
            chunk, place = chunk_of(block)
            for d, g_ref in enumerate((g0, g1, g2, g3)):

                @pl.when(chunk == d)
                def _():
                    to_ref[here, :] = g_ref[rows_at(place), :].astype(F32)

        def pick_flag(at):
            chunk, place = chunk_of(at)
            return flag_ref[pl.ds(chunk * FLAGS + place, 1), :]

        leave(shift, t_ref, pick_panel, pick_flag, y_ref, c_ref, out_ref, ys_ref, gs_ref)

    return local_call(
        kernel,
        [LEAVING] + ([in_smem(1)] if first else []),
        [coeffs, *chunks, refl],
        [table],
        scratch=GATHERED + [pltpu.VMEM((FRONTS * FLAGS, COLS), F32)],
    )


def leaf_apply(coeffs, chunks, refl):
    per = CHUNK // TILE
    blocks = TILE // BLOCK

    def kernel(c_ref, g0, g1, g2, g3, y_ref, out_far, new_ref, sems):
        def leaving(d, i):
            return pltpu.make_async_copy(
                new_ref.at[pl.ds((d * per + i) * TILE, TILE)],
                out_far.at[rows_at(ring_index(-d) * CAP + i * blocks, blocks)],
                sems.at[d * per + i],
            )

        for d, g_ref in enumerate((g0, g1, g2, g3)):
            flags = g_ref[CHUNK:, :].astype(F32)
            for i in range(per):
                rows = rows_at(ring_index(-d) * CAP + i * blocks, blocks)
                update = times_coeffs(y_ref[rows, :], c_ref[...])
                for b in range(blocks):
                    p = i * blocks + b
                    old = g_ref[p * BLOCK : (p + 1) * BLOCK, :].astype(F32)
                    new = (old - update[b * BLOCK : (b + 1) * BLOCK, :]) * flags[p : p + 1, :]
                    at = d * CHUNK + p * BLOCK
                    new_ref[at : at + BLOCK, :] = new.astype(BF16)
                leaving(d, i).start()
        for d in range(FRONTS):
            for i in range(per):
                leaving(d, i).wait()

    return local_call(
        kernel,
        [(HBM, jax.ShapeDtypeStruct((FRONTS * CHUNK, COLS), BF16))],
        [coeffs, *chunks, refl],
        scratch=[pltpu.VMEM((FRONTS * CHUNK, COLS), BF16), DMA((FRONTS * per,))],
    )[0]


def all_to_all(x, axes):
    return lax.all_to_all(x, axes, 0, 0, tiled=True)


def shifted(x, d):
    return lax.ppermute(x, "front", [(i, (i + d) % FRONTS) for i in range(FRONTS)])


ORDER = (2, 1, 3)


def route(leaving):
    chunks = {}
    for d in ORDER + (0,):
        out = leaving(d)
        chunks[d] = shifted(out, d) if d else out
    return [chunks[d] for d in range(FRONTS)]


def front_level(chunks, refl, triangle):
    total = front_partial({0: chunks[0]}, refl, None, False)
    total = front_partial({1: chunks[1], 3: chunks[3]}, refl, total, False)
    partial = front_partial({2: chunks[2]}, refl, total, True)
    arrived = all_to_all(partial.reshape(32, COLS // 32, REFL), ROWS)
    return all_to_all(front_share(arrived, triangle), ROWS).reshape(COLS, REFL)


def per_device(
    panel_g, refl_root, refl_mid, refl_leaf, tri_root, tri_mid, tri_leaf, route_root, route_mid
):
    panel = panel_g.reshape(-1, COLS)
    y_root, y_mid, y_leaf = (y.reshape(-1, REFL) for y in (refl_root, refl_mid, refl_leaf))

    partial, panel, y_root, root_table, mid_table = root_partial(
        panel, y_root, route_root.reshape(-1), route_mid.reshape(-1)
    )
    arrived = all_to_all(partial.reshape(128, 8, 128), ALL)
    coeffs = all_to_all(root_share(arrived, tri_root), ALL).reshape(COLS * 4, 128)
    token = None

    def from_root(d):
        nonlocal coeffs, token
        out = root_leave(d, coeffs, panel, y_root, root_table, token is None)
        if token is None:
            _, coeffs, token = out
        return out[0]

    chunks = route(from_root)
    y_mid = staged(y_mid, token)
    coeffs = front_level(chunks, y_mid, tri_mid[0])
    arrived, token = chunks, None

    def from_middle(d):
        nonlocal token
        out = front_leave(d, coeffs, arrived, y_mid, mid_table, token is None)
        if token is None:
            token = out[1]
        return out[0]

    chunks = route(from_middle)
    y_leaf = staged(y_leaf, token)
    coeffs = front_level(chunks, y_leaf, tri_leaf[0])
    out = leaf_apply(coeffs, chunks, y_leaf)
    return out.reshape(refl_leaf.shape[:3] + (COLS,))


def solution(mesh):
    finer = Mesh(
        mesh.devices.reshape(mesh.shape["front"], 4, 4, 2), ("front", "rows_0", "rows_1", "rows_2")
    )
    rows = P("front", ROWS, None, None)
    placed = (
        rows,
        rows,
        rows,
        rows,
        P(),
        P("front", None, None),
        P("front", None, None),
        P("front", ROWS, None),
        P("front", ROWS, None),
    )
    return jax.shard_map(
        per_device,
        mesh=finer,
        in_specs=placed,
        out_specs=rows,
        check_vma=False,
    )
```

time: 161 us -> 156 us (0.969)
  blocking collectives: 148 us -> 91.4 us
  waiting for transfers between devices: 0 us -> 31.8 us
  Pallas kernels: 12.4 us -> 25.5 us
  starting transfers between devices: 0 us -> 6.82 us
    all_to_all x8 -> x6, blocking collectives: 148 us -> 91.4 us  [all_to_all(): return lax.all_to_all(x, axes, 0, 0, tiled=True)]
    ppermute x0 -> x6, waiting for transfers between devices: none -> 31.8 us  [shifted(): lax.ppermute(x, 'front', [(i, (i + d) % FRONTS) for i in range(FRONTS)])]
    pallas_call x9 -> x21, Pallas kernels: 12.4 us -> 25.5 us  [local_call(): pl.pallas_call(kernel, in_specs=[SMEM] * len(numbers) + [VMEM] * len(held...]
    ppermute x0 -> x6, starting transfers between devices: none -> 6.82 us  [shifted(): lax.ppermute(x, 'front', [(i, (i + d) % FRONTS) for i in range(FRONTS)])]
  transfers between devices with their start and end apart: 0 -> 6, of which waited for: 0 -> 5; matrix products, arithmetic and copies ran while one was open for 0% -> 0% of each run, Pallas kernels for 0% -> 9%
where the time goes in v1:
time: 156 us
  blocking collectives  91.4 us (59%)
  waiting for transfers between devices  31.8 us (20%)
  Pallas kernels  25.5 us (16%)
  starting transfers between devices  6.82 us (4%)
    all_to_all x6, blocking collectives, all_to_all(): return lax.all_to_all(x, axes, 0, 0, tiled=True)  91.4 us
    ppermute x6, waiting for transfers between devices, shifted(): lax.ppermute(x, 'front', [(i, (i + d) % FRONTS) for i in range(FRONTS)])  31.8 us
    pallas_call x21, Pallas kernels, local_call(): pl.pallas_call(kernel, in_specs=[SMEM] * len(numbers) + [VMEM] * len(held...  25.5 us
    ppermute x6, starting transfers between devices, shifted(): lax.ppermute(x, 'front', [(i, (i + d) % FRONTS) for i in range(FRONTS)])  6.82 us
  transfers between devices with their start and end apart: 6, of which 5 were waited for; matrix products, arithmetic and copies ran while one was open for 0% of the time, Pallas kernels for 9%

profile of v1, /device:TPU:1, one launch (start us, length us, event | category | flops | bytes accessed | tf_op | source)
XLA Modules:
  0.0 155.9 jit_solution(2757116575456186929)
XLA Ops:
  0.0 0.0 copy-start
  0.0 2.8 %shard_map.91 = (bf16[1024,128]{1,0:T(8,128)(2,1)S(1)}, bf16[2048,256]{1,0:T(8,128)(2,1)S(1)}, bf16[2048,512]{1,0:T(8,128)(2,1)S(1)}, s32[32]{0:T(128)S(1)}, s32[32]{0:T(128)S(1)}) custom-call(bf16[2048,256]{1,0:T(8,128)(2,1)} %bitcast.29, bf16[2048,512]{1,0:T(8,128)(2,1)} %bitcast.28, s32[16]{0:T(128)} %bitcast.30, s32[32]{0:T(128)} %bitcast.31), custom_call_target="tpu_custom_call" | custom-call | tf_op jit(solution)/shard_map/pallas_call | solution.py:41
  2.8 22.2 %all_to_all.30.x_ref = bf16[128,8,128]{2,1,0:T(8,128)(2,1)S(1)} all-to-all(bf16[128,8,128]{2,1,0:T(8,128)(2,1)S(1)} %bitcast.25), channel_id=1, replica_groups=mesh['front'=4,'rows_0'=4,'rows_1'=4,'rows_2'=2] {'front','rows_0','rows..., dimensions={0} | all-to-all | bytes 524288 | tf_op jit(solution)/shard_map/all_to_all | solution.py:332
  24.9 0.0 copy-done
  24.9 0.5 shard_map.92
  25.4 15.3 %all_to_all.31 = bf16[128,8,128]{2,1,0:T(8,128)(2,1)S(1)} all-to-all(bf16[128,8,128]{2,1,0:T(8,128)(2,1)S(1)} %shard_map.92), channel_id=1, replica_groups=mesh['front'=4,'rows_0'=4,'rows_1'=4,'rows_2'=2] {'front','rows_0','rows..., dimensions={0} | all-to-all | bytes 524288 | tf_op jit(solution)/shard_map/all_to_all | solution.py:332
  40.7 1.3 shard_map.93
  42.1 1.0 shard_map.95
  43.1 1.0 shard_map.94
  44.1 0.3 collective-permute-start.1
  44.5 2.4 %collective-permute-start.2 = (bf16[1040,256]{1,0:T(8,128)(2,1)S(1)}, bf16[1040,256]{1,0:T(8,128)(2,1)S(1)}, u32[]{:S(2)}, u32[]{:S(2)}) collective-permute-start(bf16[1040,256]{1,0:T(8,128)(2,1)S(1)} %shard_map.95), channel_id=1, source_target_pairs={{0,96},{32,0},{64,32},{96,64},{1,97},{33,1},{65,33},{97,65},{2,98}... | collective-permute-start | bytes 1597448 | tf_op jit(solution)/shard_map/ppermute | solution.py:336
  46.9 0.0 collective-permute-start
  46.9 1.0 shard_map.96.refs_0_.g0
  47.9 2.8 %shard_map.97.refs_1_.refs_3_.refs_2_.y_ref = bf16[4096,512]{1,0:T(8,128)(2,1)S(1)} custom-call(s32[1]{0:T(128)} %get-tuple-element.22.after_ref, bf16[4096,512]{1,0:T(8,128)(2,1)} %bitcast.26), custom_call_target="tpu_custom_call" | custom-call | tf_op jit(solution)/shard_map/pallas_call | solution.py:41
  50.7 0.5 shard_map.98.refs_2_
  51.2 7.6 %collective-permute-done.1.refs_0_.g1 = bf16[1040,256]{1,0:T(8,128)(2,1)S(1)} collective-permute-done((bf16[1040,256]{1,0:T(8,128)(2,1)S(1)}, bf16[1040,256]{1,0:T(8,128)(2,1)S(1)}, u32[]{:S(2)}, u32[]{:S(2)}) %collective-permute-start.1) | collective-permute-done | bytes 532512 | tf_op jit(solution)/shard_map/ppermute | solution.py:336
  58.8 0.0 collective-permute-done.2.refs_1_.g3
  58.8 0.7 shard_map.99.refs_1_
  59.6 0.0 copy-start.1
  59.6 9.4 %collective-permute-done.refs_0_.g2 = bf16[1040,256]{1,0:T(8,128)(2,1)S(1)} collective-permute-done((bf16[1040,256]{1,0:T(8,128)(2,1)S(1)}, bf16[1040,256]{1,0:T(8,128)(2,1)S(1)}, u32[]{:S(2)}, u32[]{:S(2)}) %collective-permute-start) | collective-permute-done | bytes 532512 | tf_op jit(solution)/shard_map/ppermute | solution.py:336
  69.0 0.5 shard_map.100
  69.4 15.6 %all_to_all.32.x_ref = bf16[32,8,512]{2,1,0:T(8,128)(2,1)S(1)} all-to-all(bf16[32,8,512]{2,1,0:T(8,128)(2,1)S(1)} %bitcast.23), channel_id=1, replica_groups=mesh['front'=4,'rows_0'=4,'rows_1'=4,'rows_2'=2] {'rows_0','rows_1','row..., dimensions={0} | all-to-all | bytes 524288 | tf_op jit(solution)/shard_map/all_to_all | solution.py:332
  85.1 0.0 copy-done.1
  85.1 0.4 shard_map.101
  85.5 12.4 %all_to_all.33 = bf16[32,8,512]{2,1,0:T(8,128)(2,1)S(1)} all-to-all(bf16[32,8,512]{2,1,0:T(8,128)(2,1)S(1)} %shard_map.101), channel_id=1, replica_groups=mesh['front'=4,'rows_0'=4,'rows_1'=4,'rows_2'=2] {'rows_0','rows_1','row..., dimensions={0} | all-to-all | bytes 524288 | tf_op jit(solution)/shard_map/all_to_all | solution.py:332
  97.9 1.4 shard_map.103
  99.3 0.1 collective-permute-start.4
  99.4 1.4 shard_map.104
  100.8 2.7 %collective-permute-start.5 = (bf16[1040,256]{1,0:T(8,128)(2,1)S(1)}, bf16[1040,256]{1,0:T(8,128)(2,1)S(1)}, u32[]{:S(2)}, u32[]{:S(2)}) collective-permute-start(bf16[1040,256]{1,0:T(8,128)(2,1)S(1)} %shard_map.104), channel_id=1, source_target_pairs={{0,96},{32,0},{64,32},{96,64},{1,97},{33,1},{65,33},{97,65},{2,98}... | collective-permute-start | bytes 1597448 | tf_op jit(solution)/shard_map/ppermute | solution.py:336
  103.5 1.4 shard_map.102
  105.0 1.2 collective-permute-start.3
  106.2 2.8 %shard_map.106.refs_1_.refs_3_.refs_2_.y_ref = bf16[4096,512]{1,0:T(8,128)(2,1)S(1)} custom-call(s32[1]{0:T(128)} %get-tuple-element.24.after_ref, bf16[4096,512]{1,0:T(8,128)(2,1)} %bitcast.27), custom_call_target="tpu_custom_call" | custom-call | tf_op jit(solution)/shard_map/pallas_call | solution.py:41
  109.1 1.6 %shard_map.105.refs_0_.g0 = bf16[1040,256]{1,0:T(8,128)(2,1)S(1)} custom-call(s32[32]{0:T(128)S(1)} %get-tuple-element.15.t_ref, bf16[256,512]{1,0:T(8,128)(2,1)S(1)} %bitcast.18, bf16[1040,256]{1,0:T(8,128)(2,1)S(1)} %shard_map.96.refs_0_.g0, bf16[1040,256]{1,0:T(8,128)(2,1)S(1)} %collective-permute-done.1.refs_0_.g1, ...), custom_call_target="tpu_custom_call" | custom-call | tf_op jit(solution)/shard_map/pallas_call | solution.py:41
  110.6 0.5 shard_map.107.refs_2_
  111.1 3.0 %collective-permute-done.4.refs_0_.g1 = bf16[1040,256]{1,0:T(8,128)(2,1)S(1)} collective-permute-done((bf16[1040,256]{1,0:T(8,128)(2,1)S(1)}, bf16[1040,256]{1,0:T(8,128)(2,1)S(1)}, u32[]{:S(2)}, u32[]{:S(2)}) %collective-permute-start.4) | collective-permute-done | bytes 532512 | tf_op jit(solution)/shard_map/ppermute | solution.py:336
  114.1 11.7 %collective-permute-done.5.refs_1_.g3 = bf16[1040,256]{1,0:T(8,128)(2,1)S(1)} collective-permute-done((bf16[1040,256]{1,0:T(8,128)(2,1)S(1)}, bf16[1040,256]{1,0:T(8,128)(2,1)S(1)}, u32[]{:S(2)}, u32[]{:S(2)}) %collective-permute-start.5) | collective-permute-done | bytes 532512 | tf_op jit(solution)/shard_map/ppermute | solution.py:336
  125.8 0.7 shard_map.108.refs_1_
  126.6 0.0 copy-start.2
  126.6 0.1 collective-permute-done.3.refs_0_.g2
  126.7 0.5 shard_map.109
  127.1 13.5 %all_to_all.34.x_ref = bf16[32,8,512]{2,1,0:T(8,128)(2,1)S(1)} all-to-all(bf16[32,8,512]{2,1,0:T(8,128)(2,1)S(1)} %bitcast.24), channel_id=1, replica_groups=mesh['front'=4,'rows_0'=4,'rows_1'=4,'rows_2'=2] {'rows_0','rows_1','row..., dimensions={0} | all-to-all | bytes 524288 | tf_op jit(solution)/shard_map/all_to_all | solution.py:332
  140.6 0.0 copy-done.2
  140.6 0.4 shard_map.110
  141.0 12.4 %all_to_all.35 = bf16[32,8,512]{2,1,0:T(8,128)(2,1)S(1)} all-to-all(bf16[32,8,512]{2,1,0:T(8,128)(2,1)S(1)} %shard_map.110), channel_id=1, replica_groups=mesh['front'=4,'rows_0'=4,'rows_1'=4,'rows_2'=2] {'rows_0','rows_1','row..., dimensions={0} | all-to-all | bytes 524288 | tf_op jit(solution)/shard_map/all_to_all | solution.py:332
  153.5 2.2 %shard_map.111 = bf16[4096,256]{1,0:T(8,128)(2,1)} custom-call(bf16[256,512]{1,0:T(8,128)(2,1)S(1)} %bitcast.19, bf16[1040,256]{1,0:T(8,128)(2,1)S(1)} %shard_map.105.refs_0_.g0, bf16[1040,256]{1,0:T(8,128)(2,1)S(1)} %collective-permute-done.4.refs_0_.g1, bf16[1040,256]{1,0:T(8,128)(2,1)S(1)} %collective-permute-done.3.refs_0_.g2, ...), custom_call_target="tpu_custom_call" | custom-call | tf_op jit(solution)/shard_map/pallas_call | solution.py:41
Async XLA Ops:
  0.0 24.9 %copy-start = (f32[512,512]{1,0:T(8,128)S(1)}, f32[512,512]{1,0:T(8,128)}, u32[]{:S(2)}) copy-start(f32[512,512]{1,0:T(8,128)} %t_ref.1) | copy-start | bytes 3145732
  44.1 14.7 %collective-permute-start.1 = (bf16[1040,256]{1,0:T(8,128)(2,1)S(1)}, bf16[1040,256]{1,0:T(8,128)(2,1)S(1)}, u32[]{:S(2)}, u32[]{:S(2)}) collective-permute-start(bf16[1040,256]{1,0:T(8,128)(2,1)S(1)} %shard_map.94), channel_id=1, source_target_pairs={{0,32},{32,64},{64,96},{96,0},{1,33},{33,65},{65,97},{97,1},{2,34}... | collective-permute-start | bytes 1597448 | tf_op jit(solution)/shard_map/ppermute | solution.py:336
  44.5 14.4 %collective-permute-start.2 = (bf16[1040,256]{1,0:T(8,128)(2,1)S(1)}, bf16[1040,256]{1,0:T(8,128)(2,1)S(1)}, u32[]{:S(2)}, u32[]{:S(2)}) collective-permute-start(bf16[1040,256]{1,0:T(8,128)(2,1)S(1)} %shard_map.95), channel_id=1, source_target_pairs={{0,96},{32,0},{64,32},{96,64},{1,97},{33,1},{65,33},{97,65},{2,98}... | collective-permute-start | bytes 1597448 | tf_op jit(solution)/shard_map/ppermute | solution.py:336
  46.9 22.1 %collective-permute-start = (bf16[1040,256]{1,0:T(8,128)(2,1)S(1)}, bf16[1040,256]{1,0:T(8,128)(2,1)S(1)}, u32[]{:S(2)}, u32[]{:S(2)}) collective-permute-start(bf16[1040,256]{1,0:T(8,128)(2,1)S(1)} %get-tuple-element.20), channel_id=1, source_target_pairs={{0,64},{32,96},{64,0},{96,32},{1,65},{33,97},{65,1},{97,33},{2,66}... | collective-permute-start | bytes 1597448 | tf_op jit(solution)/shard_map/ppermute | solution.py:336
  59.6 25.5 %copy-start.1 = (f32[1,512,512]{2,1,0:T(8,128)S(1)}, f32[1,512,512]{2,1,0:T(8,128)}, u32[]{:S(2)}) copy-start(f32[1,512,512]{2,1,0:T(8,128)} %param.14) | copy-start | bytes 3145732
  99.3 14.8 %collective-permute-start.4 = (bf16[1040,256]{1,0:T(8,128)(2,1)S(1)}, bf16[1040,256]{1,0:T(8,128)(2,1)S(1)}, u32[]{:S(2)}, u32[]{:S(2)}) collective-permute-start(bf16[1040,256]{1,0:T(8,128)(2,1)S(1)} %shard_map.103), channel_id=1, source_target_pairs={{0,32},{32,64},{64,96},{96,0},{1,33},{33,65},{65,97},{97,1},{2,34}... | collective-permute-start | bytes 1597448 | tf_op jit(solution)/shard_map/ppermute | solution.py:336
  100.8 25.0 %collective-permute-start.5 = (bf16[1040,256]{1,0:T(8,128)(2,1)S(1)}, bf16[1040,256]{1,0:T(8,128)(2,1)S(1)}, u32[]{:S(2)}, u32[]{:S(2)}) collective-permute-start(bf16[1040,256]{1,0:T(8,128)(2,1)S(1)} %shard_map.104), channel_id=1, source_target_pairs={{0,96},{32,0},{64,32},{96,64},{1,97},{33,1},{65,33},{97,65},{2,98}... | collective-permute-start | bytes 1597448 | tf_op jit(solution)/shard_map/ppermute | solution.py:336
  105.0 21.7 %collective-permute-start.3 = (bf16[1040,256]{1,0:T(8,128)(2,1)S(1)}, bf16[1040,256]{1,0:T(8,128)(2,1)S(1)}, u32[]{:S(2)}, u32[]{:S(2)}) collective-permute-start(bf16[1040,256]{1,0:T(8,128)(2,1)S(1)} %get-tuple-element.23), channel_id=1, source_target_pairs={{0,64},{32,96},{64,0},{96,32},{1,65},{33,97},{65,1},{97,33},{2,66}... | collective-permute-start | bytes 1597448 | tf_op jit(solution)/shard_map/ppermute | solution.py:336
  126.6 14.0 %copy-start.2 = (f32[1,512,512]{2,1,0:T(8,128)S(1)}, f32[1,512,512]{2,1,0:T(8,128)}, u32[]{:S(2)}) copy-start(f32[1,512,512]{2,1,0:T(8,128)} %param.15) | copy-start | bytes 3145732

commit v2 on v1

--- a/solution.py
+++ b/solution.py
@@ -348,9 +348,9 @@
 
 
 def front_level(chunks, refl, triangle):
-    total = front_partial({0: chunks[0]}, refl, None, False)
-    total = front_partial({1: chunks[1], 3: chunks[3]}, refl, total, False)
-    partial = front_partial({2: chunks[2]}, refl, total, True)
+    partial = None
+    for d in (0,) + ORDER:
+        partial = front_partial({d: chunks[d]}, refl, partial, d == ORDER[-1])
     arrived = all_to_all(partial.reshape(32, COLS // 32, REFL), ROWS)
     return all_to_all(front_share(arrived, triangle), ROWS).reshape(COLS, REFL)
 

time: 156 us -> 154 us (0.987)
  blocking collectives: 91.4 us -> 87.9 us
    all_to_all x6, blocking collectives: 91.4 us -> 87.9 us  [all_to_all(): return lax.all_to_all(x, axes, 0, 0, tiled=True)]
    pallas_call x21 -> x23, Pallas kernels: 25.5 us -> 25.8 us  [local_call(): pl.pallas_call(kernel, in_specs=[SMEM] * len(numbers) + [VMEM] * len(held...]
  transfers between devices with their start and end apart: 6 -> 6, of which waited for: 5 -> 4; matrix products, arithmetic and copies ran while one was open for 0% -> 0% of each run, Pallas kernels for 9% -> 10%
where the time goes in v2:
time: 154 us; the launch traced here: 153 us
  blocking collectives  87.9 us (57%)
  waiting for transfers between devices  31.4 us (20%)
  Pallas kernels  25.8 us (17%)
  starting transfers between devices  7.64 us (5%)
    all_to_all x6, blocking collectives, all_to_all(): return lax.all_to_all(x, axes, 0, 0, tiled=True)  87.9 us
    ppermute x6, waiting for transfers between devices, shifted(): lax.ppermute(x, 'front', [(i, (i + d) % FRONTS) for i in range(FRONTS)])  31.4 us
    pallas_call x23, Pallas kernels, local_call(): pl.pallas_call(kernel, in_specs=[SMEM] * len(numbers) + [VMEM] * len(held...  25.8 us
    ppermute x6, starting transfers between devices, shifted(): lax.ppermute(x, 'front', [(i, (i + d) % FRONTS) for i in range(FRONTS)])  7.64 us
  transfers between devices with their start and end apart: 6, of which 4 were waited for; matrix products, arithmetic and copies ran while one was open for 0% of the time, Pallas kernels for 10%

profile of v2, /device:TPU:1, one launch (start us, length us, event | category | flops | bytes accessed | tf_op | source)
XLA Modules:
  0.0 153.2 jit_solution(8715884635272663686)
XLA Ops:
  0.0 0.0 copy-start
  0.0 2.8 %shard_map.91 = (bf16[1024,128]{1,0:T(8,128)(2,1)S(1)}, bf16[2048,256]{1,0:T(8,128)(2,1)S(1)}, bf16[2048,512]{1,0:T(8,128)(2,1)S(1)}, s32[32]{0:T(128)S(1)}, s32[32]{0:T(128)S(1)}) custom-call(bf16[2048,256]{1,0:T(8,128)(2,1)} %bitcast.29, bf16[2048,512]{1,0:T(8,128)(2,1)} %bitcast.28, s32[16]{0:T(128)} %bitcast.30, s32[32]{0:T(128)} %bitcast.31), custom_call_target="tpu_custom_call" | custom-call | tf_op jit(solution)/shard_map/pallas_call | solution.py:41
  2.8 22.2 %all_to_all.30.x_ref = bf16[128,8,128]{2,1,0:T(8,128)(2,1)S(1)} all-to-all(bf16[128,8,128]{2,1,0:T(8,128)(2,1)S(1)} %bitcast.25), channel_id=1, replica_groups=mesh['front'=4,'rows_0'=4,'rows_1'=4,'rows_2'=2] {'front','rows_0','rows..., dimensions={0} | all-to-all | bytes 524288 | tf_op jit(solution)/shard_map/all_to_all | solution.py:332
  24.9 0.0 copy-done
  24.9 0.5 shard_map.92
  25.4 15.3 %all_to_all.31 = bf16[128,8,128]{2,1,0:T(8,128)(2,1)S(1)} all-to-all(bf16[128,8,128]{2,1,0:T(8,128)(2,1)S(1)} %shard_map.92), channel_id=1, replica_groups=mesh['front'=4,'rows_0'=4,'rows_1'=4,'rows_2'=2] {'front','rows_0','rows..., dimensions={0} | all-to-all | bytes 524288 | tf_op jit(solution)/shard_map/all_to_all | solution.py:332
  40.7 1.3 shard_map.93
  42.1 1.3 collective-permute-start.2
  43.4 1.0 shard_map.95
  44.4 0.1 collective-permute-start.1
  44.6 1.0 shard_map.94
  45.6 2.7 %collective-permute-start = (bf16[1040,256]{1,0:T(8,128)(2,1)S(1)}, bf16[1040,256]{1,0:T(8,128)(2,1)S(1)}, u32[]{:S(2)}, u32[]{:S(2)}) collective-permute-start(bf16[1040,256]{1,0:T(8,128)(2,1)S(1)} %shard_map.94), channel_id=1, source_target_pairs={{0,96},{32,0},{64,32},{96,64},{1,97},{33,1},{65,33},{97,65},{2,98}... | collective-permute-start | bytes 1597448 | tf_op jit(solution)/shard_map/ppermute | solution.py:336
  48.2 1.0 shard_map.96.refs_0_.g0
  49.3 2.8 %shard_map.97.refs_1_.refs_2_.y_ref = bf16[4096,512]{1,0:T(8,128)(2,1)S(1)} custom-call(s32[1]{0:T(128)} %get-tuple-element.22.after_ref, bf16[4096,512]{1,0:T(8,128)(2,1)} %bitcast.26), custom_call_target="tpu_custom_call" | custom-call | tf_op jit(solution)/shard_map/pallas_call | solution.py:41
  52.1 0.5 shard_map.98.refs_1_
  52.6 3.9 %collective-permute-done.2.refs_0_.g2 = bf16[1040,256]{1,0:T(8,128)(2,1)S(1)} collective-permute-done((bf16[1040,256]{1,0:T(8,128)(2,1)S(1)}, bf16[1040,256]{1,0:T(8,128)(2,1)S(1)}, u32[]{:S(2)}, u32[]{:S(2)}) %collective-permute-start.2) | collective-permute-done | bytes 532512 | tf_op jit(solution)/shard_map/ppermute | solution.py:336
  56.5 0.5 shard_map.99.refs_1_
  56.9 12.1 %collective-permute-done.1.refs_0_.g1 = bf16[1040,256]{1,0:T(8,128)(2,1)S(1)} collective-permute-done((bf16[1040,256]{1,0:T(8,128)(2,1)S(1)}, bf16[1040,256]{1,0:T(8,128)(2,1)S(1)}, u32[]{:S(2)}, u32[]{:S(2)}) %collective-permute-start.1) | collective-permute-done | bytes 532512 | tf_op jit(solution)/shard_map/ppermute | solution.py:336
  69.1 0.5 shard_map.100.refs_1_
  69.6 0.0 copy-start.1
  69.6 0.0 collective-permute-done.refs_0_.g3
  69.6 0.5 shard_map.101
  70.1 13.0 %all_to_all.32.x_ref = bf16[32,8,512]{2,1,0:T(8,128)(2,1)S(1)} all-to-all(bf16[32,8,512]{2,1,0:T(8,128)(2,1)S(1)} %bitcast.23), channel_id=1, replica_groups=mesh['front'=4,'rows_0'=4,'rows_1'=4,'rows_2'=2] {'rows_0','rows_1','row..., dimensions={0} | all-to-all | bytes 524288 | tf_op jit(solution)/shard_map/all_to_all | solution.py:332
  83.0 0.0 copy-done.1
  83.0 0.4 shard_map.102
  83.5 12.4 %all_to_all.33 = bf16[32,8,512]{2,1,0:T(8,128)(2,1)S(1)} all-to-all(bf16[32,8,512]{2,1,0:T(8,128)(2,1)S(1)} %shard_map.102), channel_id=1, replica_groups=mesh['front'=4,'rows_0'=4,'rows_1'=4,'rows_2'=2] {'rows_0','rows_1','row..., dimensions={0} | all-to-all | bytes 524288 | tf_op jit(solution)/shard_map/all_to_all | solution.py:332
  95.9 1.4 shard_map.105
  97.4 0.7 collective-permute-start.5
  98.1 1.4 shard_map.104
  99.5 0.3 collective-permute-start.4
  99.8 1.4 shard_map.103
  101.2 2.5 %collective-permute-start.3 = (bf16[1040,256]{1,0:T(8,128)(2,1)S(1)}, bf16[1040,256]{1,0:T(8,128)(2,1)S(1)}, u32[]{:S(2)}, u32[]{:S(2)}) collective-permute-start(bf16[1040,256]{1,0:T(8,128)(2,1)S(1)} %shard_map.103), channel_id=1, source_target_pairs={{0,96},{32,0},{64,32},{96,64},{1,97},{33,1},{65,33},{97,65},{2,98}... | collective-permute-start | bytes 1597448 | tf_op jit(solution)/shard_map/ppermute | solution.py:336
  103.6 2.8 %shard_map.107.refs_1_.refs_2_.y_ref = bf16[4096,512]{1,0:T(8,128)(2,1)S(1)} custom-call(s32[1]{0:T(128)} %get-tuple-element.24.after_ref, bf16[4096,512]{1,0:T(8,128)(2,1)} %bitcast.27), custom_call_target="tpu_custom_call" | custom-call | tf_op jit(solution)/shard_map/pallas_call | solution.py:41
  106.5 1.6 %shard_map.106.refs_0_.g0 = bf16[1040,256]{1,0:T(8,128)(2,1)S(1)} custom-call(s32[32]{0:T(128)S(1)} %get-tuple-element.15.t_ref, bf16[256,512]{1,0:T(8,128)(2,1)S(1)} %bitcast.18, bf16[1040,256]{1,0:T(8,128)(2,1)S(1)} %shard_map.96.refs_0_.g0, bf16[1040,256]{1,0:T(8,128)(2,1)S(1)} %collective-permute-done.1.refs_0_.g1, ...), custom_call_target="tpu_custom_call" | custom-call | tf_op jit(solution)/shard_map/pallas_call | solution.py:41
  108.1 0.5 shard_map.108.refs_1_
  108.5 4.0 %collective-permute-done.5.refs_0_.g2 = bf16[1040,256]{1,0:T(8,128)(2,1)S(1)} collective-permute-done((bf16[1040,256]{1,0:T(8,128)(2,1)S(1)}, bf16[1040,256]{1,0:T(8,128)(2,1)S(1)}, u32[]{:S(2)}, u32[]{:S(2)}) %collective-permute-start.5) | collective-permute-done | bytes 532512 | tf_op jit(solution)/shard_map/ppermute | solution.py:336
  112.5 0.5 shard_map.109.refs_1_
  113.0 11.4 %collective-permute-done.4.refs_0_.g1 = bf16[1040,256]{1,0:T(8,128)(2,1)S(1)} collective-permute-done((bf16[1040,256]{1,0:T(8,128)(2,1)S(1)}, bf16[1040,256]{1,0:T(8,128)(2,1)S(1)}, u32[]{:S(2)}, u32[]{:S(2)}) %collective-permute-start.4) | collective-permute-done | bytes 532512 | tf_op jit(solution)/shard_map/ppermute | solution.py:336
  124.4 0.5 shard_map.110.refs_1_
  124.9 0.0 copy-start.2
  124.9 0.0 collective-permute-done.3.refs_0_.g3
  124.9 0.5 shard_map.111
  125.3 12.6 %all_to_all.34.x_ref = bf16[32,8,512]{2,1,0:T(8,128)(2,1)S(1)} all-to-all(bf16[32,8,512]{2,1,0:T(8,128)(2,1)S(1)} %bitcast.24), channel_id=1, replica_groups=mesh['front'=4,'rows_0'=4,'rows_1'=4,'rows_2'=2] {'rows_0','rows_1','row..., dimensions={0} | all-to-all | bytes 524288 | tf_op jit(solution)/shard_map/all_to_all | solution.py:332
  137.9 0.0 copy-done.2
  137.9 0.4 shard_map.112
  138.4 12.4 %all_to_all.35 = bf16[32,8,512]{2,1,0:T(8,128)(2,1)S(1)} all-to-all(bf16[32,8,512]{2,1,0:T(8,128)(2,1)S(1)} %shard_map.112), channel_id=1, replica_groups=mesh['front'=4,'rows_0'=4,'rows_1'=4,'rows_2'=2] {'rows_0','rows_1','row..., dimensions={0} | all-to-all | bytes 524288 | tf_op jit(solution)/shard_map/all_to_all | solution.py:332
  150.8 2.2 %shard_map.113 = bf16[4096,256]{1,0:T(8,128)(2,1)} custom-call(bf16[256,512]{1,0:T(8,128)(2,1)S(1)} %bitcast.19, bf16[1040,256]{1,0:T(8,128)(2,1)S(1)} %shard_map.106.refs_0_.g0, bf16[1040,256]{1,0:T(8,128)(2,1)S(1)} %collective-permute-done.4.refs_0_.g1, bf16[1040,256]{1,0:T(8,128)(2,1)S(1)} %collective-permute-done.5.refs_0_.g2, ...), custom_call_target="tpu_custom_call" | custom-call | tf_op jit(solution)/shard_map/pallas_call | solution.py:41
Async XLA Ops:
  0.0 24.9 %copy-start = (f32[512,512]{1,0:T(8,128)S(1)}, f32[512,512]{1,0:T(8,128)}, u32[]{:S(2)}) copy-start(f32[512,512]{1,0:T(8,128)} %t_ref.1) | copy-start | bytes 3145732
  42.1 14.4 %collective-permute-start.2 = (bf16[1040,256]{1,0:T(8,128)(2,1)S(1)}, bf16[1040,256]{1,0:T(8,128)(2,1)S(1)}, u32[]{:S(2)}, u32[]{:S(2)}) collective-permute-start(bf16[1040,256]{1,0:T(8,128)(2,1)S(1)} %get-tuple-element.21), channel_id=1, source_target_pairs={{0,64},{32,96},{64,0},{96,32},{1,65},{33,97},{65,1},{97,33},{2,66}... | collective-permute-start | bytes 1597448 | tf_op jit(solution)/shard_map/ppermute | solution.py:336
  44.4 24.7 %collective-permute-start.1 = (bf16[1040,256]{1,0:T(8,128)(2,1)S(1)}, bf16[1040,256]{1,0:T(8,128)(2,1)S(1)}, u32[]{:S(2)}, u32[]{:S(2)}) collective-permute-start(bf16[1040,256]{1,0:T(8,128)(2,1)S(1)} %shard_map.95), channel_id=1, source_target_pairs={{0,32},{32,64},{64,96},{96,0},{1,33},{33,65},{65,97},{97,1},{2,34}... | collective-permute-start | bytes 1597448 | tf_op jit(solution)/shard_map/ppermute | solution.py:336
  45.6 24.0 %collective-permute-start = (bf16[1040,256]{1,0:T(8,128)(2,1)S(1)}, bf16[1040,256]{1,0:T(8,128)(2,1)S(1)}, u32[]{:S(2)}, u32[]{:S(2)}) collective-permute-start(bf16[1040,256]{1,0:T(8,128)(2,1)S(1)} %shard_map.94), channel_id=1, source_target_pairs={{0,96},{32,0},{64,32},{96,64},{1,97},{33,1},{65,33},{97,65},{2,98}... | collective-permute-start | bytes 1597448 | tf_op jit(solution)/shard_map/ppermute | solution.py:336
  69.6 13.5 %copy-start.1 = (f32[1,512,512]{2,1,0:T(8,128)S(1)}, f32[1,512,512]{2,1,0:T(8,128)}, u32[]{:S(2)}) copy-start(f32[1,512,512]{2,1,0:T(8,128)} %param.14) | copy-start | bytes 3145732
  97.4 15.1 %collective-permute-start.5 = (bf16[1040,256]{1,0:T(8,128)(2,1)S(1)}, bf16[1040,256]{1,0:T(8,128)(2,1)S(1)}, u32[]{:S(2)}, u32[]{:S(2)}) collective-permute-start(bf16[1040,256]{1,0:T(8,128)(2,1)S(1)} %get-tuple-element.23), channel_id=1, source_target_pairs={{0,64},{32,96},{64,0},{96,32},{1,65},{33,97},{65,1},{97,33},{2,66}... | collective-permute-start | bytes 1597448 | tf_op jit(solution)/shard_map/ppermute | solution.py:336
  99.5 24.9 %collective-permute-start.4 = (bf16[1040,256]{1,0:T(8,128)(2,1)S(1)}, bf16[1040,256]{1,0:T(8,128)(2,1)S(1)}, u32[]{:S(2)}, u32[]{:S(2)}) collective-permute-start(bf16[1040,256]{1,0:T(8,128)(2,1)S(1)} %shard_map.104), channel_id=1, source_target_pairs={{0,32},{32,64},{64,96},{96,0},{1,33},{33,65},{65,97},{97,1},{2,34}... | collective-permute-start | bytes 1597448 | tf_op jit(solution)/shard_map/ppermute | solution.py:336
  101.2 23.7 %collective-permute-start.3 = (bf16[1040,256]{1,0:T(8,128)(2,1)S(1)}, bf16[1040,256]{1,0:T(8,128)(2,1)S(1)}, u32[]{:S(2)}, u32[]{:S(2)}) collective-permute-start(bf16[1040,256]{1,0:T(8,128)(2,1)S(1)} %shard_map.103), channel_id=1, source_target_pairs={{0,96},{32,0},{64,32},{96,64},{1,97},{33,1},{65,33},{97,65},{2,98}... | collective-permute-start | bytes 1597448 | tf_op jit(solution)/shard_map/ppermute | solution.py:336
  124.9 13.1 %copy-start.2 = (f32[1,512,512]{2,1,0:T(8,128)S(1)}, f32[1,512,512]{2,1,0:T(8,128)}, u32[]{:S(2)}) copy-start(f32[1,512,512]{2,1,0:T(8,128)} %param.15) | copy-start | bytes 3145732
